TPU v7x, 32 devices: a whole 2x2x4 slice. The times are simulated.
32 devices in a mesh: gz: 4 (over z), gy: 8 (over y, x, core).
Axes of the slice: x: 2, y: 2, z: 4, core: 2. Of those that a mesh axis runs over, the one named last changes fastest.
Arguments:
- vel_pre: float32 [3, 192, 1024, 128], P(None, 'gz', 'gy')
- vel_farm: float32 [3, 192, 1024, 384], P(None, 'gz', 'gy')
- thrust: float32 [8], replicated, may hold values from 1 to 4
- turbine_cells: int32 [3, 8, 64], replicated, may hold values from 0 to 1023, as said below
- inflow_rows: int32 [1024], P('gy'), may hold values from 0 to 1023
Outputs:
- new_pre: float32 [3, 192, 1024, 128], P(None, 'gz', 'gy')
- new_farm: float32 [3, 192, 1024, 384], P(None, 'gz', 'gy')
Inputs may be any that keep to these rules, and one draw needn't show every extreme that they name: turbine_cells[0], [1], [2] hold z, y, x; the 64 cells of turbine t are z0 + i, y0 + j (0 <= i, j < 8) at one x; the turbines stand in four streamwise rows, several turbines may share a row.
All inputs are finite; a program needn't handle non-finite values.
Results may differ from a plain program's by a relative error of at most 0.0003.
Values sent between devices are 32-bit elements; how exact they have to be, the bound alone decides.
A program may use at most 640 MiB of HBM per device.

v0:
```python
import jax
import jax.numpy as jnp
from jax import lax
from jax.sharding import PartitionSpec as P

FRINGE = 32


time_step = 0.1
viscosity = 0.05
smagorinsky = 0.03
highest = lax.Precision.HIGHEST


def shifted(block, axis, distance):
    devices = range(lax.axis_size(axis))
    route = [((i - distance) % len(devices), i) for i in devices]
    return lax.ppermute(block, axis, route)


def shifted_2(value, axis, steps):
    count = lax.axis_size(axis)
    first, last = (max(0, -steps), min(count, count - steps))
    return lax.ppermute(value, axis, [(source, source + steps) for source in range(first, last)])


def tendency(velocity, up_x, dn_x, up_y, dn_y, up_z, dn_z):
    grad_x = 0.5 * (up_x - dn_x)
    grad_y = 0.5 * (up_y - dn_y)
    grad_z = 0.5 * (up_z - dn_z)
    laplace = up_x + dn_x + up_y + dn_y + up_z + dn_z - 6.0 * velocity
    advect = velocity[0:1] * grad_x + velocity[1:2] * grad_y + velocity[2:3] * grad_z
    shear_sq = 2.0 * (grad_x[0] * grad_x[0] + grad_y[1] * grad_y[1] + grad_z[2] * grad_z[2])
    shear_sq = shear_sq + (grad_y[0] + grad_x[1]) * (grad_y[0] + grad_x[1])
    shear_sq = shear_sq + (grad_z[0] + grad_x[2]) * (grad_z[0] + grad_x[2])
    shear_sq = shear_sq + (grad_z[1] + grad_y[2]) * (grad_z[1] + grad_y[2])
    eddy_visc = viscosity + smagorinsky * jnp.sqrt(shear_sq)
    return velocity + time_step * (eddy_visc * laplace - advect)


def span_neighbor(planes, offset):
    return shifted(planes, "gy", offset)


def vertical_neighbor(planes, offset):
    return shifted_2(planes, "gz", offset)


def dct_tables(count):
    integer_ids = jnp.arange(count, dtype=jnp.int32)
    phases = integer_ids[:, None] * (2 * integer_ids[None, :] + 1) % (4 * count)
    forward = jnp.cos(jnp.pi * phases.astype(jnp.float32) / (2 * count))
    weights = jnp.where(integer_ids == 0, 1.0, 2.0).astype(jnp.float32) / count
    inverse = forward.T * weights[None, :]
    return (forward, inverse)


def cas_square(count):
    integer_ids = jnp.arange(count, dtype=jnp.int32)
    phases = integer_ids[:, None] * integer_ids[None, :] % count
    angles = 2.0 * jnp.pi * phases.astype(jnp.float32) / count
    return jnp.cos(angles) + jnp.sin(angles)


def hartley_x(mode_ids, cell_ids, len_pre, len_farm, inverse):
    mode_farm = mode_ids >= len_pre
    cell_farm = cell_ids >= len_pre
    wavenum = jnp.where(mode_farm, mode_ids - len_pre, mode_ids)
    places = jnp.where(cell_farm, cell_ids - len_pre, cell_ids)
    length = jnp.where(mode_farm, len_farm, len_pre)
    phases = wavenum[:, None] * places[None, :] % length[:, None]
    angles = 2.0 * jnp.pi * phases.astype(jnp.float32) / length[:, None].astype(jnp.float32)
    same_domain = (mode_farm[:, None] == cell_farm[None, :]).astype(jnp.float32)
    matrix = (jnp.cos(angles) + jnp.sin(angles)) * same_domain
    if inverse:
        matrix = matrix / length[:, None].astype(jnp.float32)
    return matrix


def eigen(wavenum, length):
    sine_val = jnp.sin(jnp.pi * wavenum.astype(jnp.float32) / length)
    return 4.0 * sine_val * sine_val


def solve_modes(spectrum, kx_modes, ky_waves, len_pre, len_farm, total_y):
    depth_all = spectrum.shape[0]
    wave_z = jnp.arange(depth_all, dtype=jnp.int32)
    mode_farm = kx_modes >= len_pre
    wavenum = jnp.where(mode_farm, kx_modes - len_pre, kx_modes)
    length = jnp.where(mode_farm, len_farm, len_pre).astype(jnp.float32)
    sine_val = jnp.sin(jnp.pi * wavenum.astype(jnp.float32) / length)
    rate_x = 4.0 * sine_val * sine_val
    summed = (
        eigen(wave_z, 2 * depth_all)[:, None, None]
        + rate_x[None, :, None]
        + eigen(ky_waves, total_y)[None, None, :]
    )
    null_mode = (
        (wave_z[:, None, None] == 0)
        & (wavenum[None, :, None] == 0)
        & (ky_waves[None, None, :] == 0)
    )
    return jnp.where(null_mode, 0.0, -spectrum / jnp.where(null_mode, 1.0, summed))


def body(vel_pre, vel_farm, thrust, turbine_cells, inflow_rows):
    count_z = lax.axis_size("gz")
    count_y = lax.axis_size("gy")
    zone_z = lax.axis_index("gz")
    zone_y = lax.axis_index("gy")
    depth = vel_pre.shape[1]
    span = vel_pre.shape[2]
    len_pre = vel_pre.shape[3]
    len_farm = vel_farm.shape[3]
    total_z = depth * count_z
    total_y = span * count_y
    modes = len_pre + len_farm
    low_y = span_neighbor(jnp.concatenate([vel_pre[:, :, -1:], vel_farm[:, :, -1:]], -1), 1)
    high_y = span_neighbor(jnp.concatenate([vel_pre[:, :, :1], vel_farm[:, :, :1]], -1), -1)
    low_z = vertical_neighbor(jnp.concatenate([vel_pre[:, -1:], vel_farm[:, -1:]], -1), 1)
    high_z = vertical_neighbor(jnp.concatenate([vel_pre[:, :1], vel_farm[:, :1]], -1), -1)

    def predict(velocity, first_col, last_col):
        up_y = jnp.concatenate([velocity[:, :, 1:], high_y[..., first_col:last_col]], 2)
        dn_y = jnp.concatenate([low_y[..., first_col:last_col], velocity[:, :, :-1]], 2)
        up_z = jnp.concatenate([velocity[:, 1:], high_z[..., first_col:last_col]], 1)
        dn_z = jnp.concatenate([low_z[..., first_col:last_col], velocity[:, :-1]], 1)
        return tendency(
            velocity, jnp.roll(velocity, -1, 3), jnp.roll(velocity, 1, 3), up_y, dn_y, up_z, dn_z
        )

    star_pre = predict(vel_pre, 0, len_pre)
    star_farm = predict(vel_farm, len_pre, modes)
    cell_z = turbine_cells[0] - zone_z * depth
    cell_y = turbine_cells[1] - zone_y * span
    cell_x = turbine_cells[2]
    inside = (cell_z >= 0) & (cell_z < depth) & (cell_y >= 0) & (cell_y < span)
    flat_cell = jnp.where(inside, (cell_z * span + cell_y) * len_farm + cell_x, 0).reshape(-1)
    stream_vel = vel_farm[0].reshape(-1)[flat_cell].reshape(inside.shape)
    thrust_force = jnp.where(
        inside, -time_step * thrust[:, None] * jnp.abs(stream_vel) * stream_vel, 0.0
    )
    stream_new = (
        star_farm[0]
        .reshape(-1)
        .at[flat_cell]
        .add(thrust_force.reshape(-1))
        .reshape(depth, span, len_farm)
    )
    star_farm = jnp.concatenate([stream_new[None], star_farm[1:]], 0)
    outlet = vel_pre[:, :, :, -1]
    whole_plane = lax.all_gather(outlet, "gy", axis=2, tiled=True)
    inflow = jnp.take(whole_plane, inflow_rows, axis=2)
    weight = (
        jnp.maximum(FRINGE - jnp.arange(len_farm, dtype=jnp.int32), 0).astype(jnp.float32) / FRINGE
    )
    star_farm = star_farm + weight * (inflow[..., None] - star_farm)
    z_global = zone_z * depth + jnp.arange(depth, dtype=jnp.int32)
    below_top = (z_global < total_z - 1).astype(jnp.float32)
    lid_mask = jnp.stack([jnp.ones_like(below_top), jnp.ones_like(below_top), below_top])[
        :, :, None, None
    ]
    star_pre = star_pre * lid_mask
    star_farm = star_farm * lid_mask
    low_north = span_neighbor(jnp.concatenate([star_pre[1, :, -1:], star_farm[1, :, -1:]], -1), 1)
    low_up = vertical_neighbor(jnp.concatenate([star_pre[2, -1:], star_farm[2, -1:]], -1), 1)

    def divergence_of(star, first_col, last_col):
        east_vel, north_vel, upward_vel = (star[0], star[1], star[2])
        dn_north = jnp.concatenate([low_north[..., first_col:last_col], north_vel[:, :-1]], 1)
        dn_up = jnp.concatenate([low_up[..., first_col:last_col], upward_vel[:-1]], 0)
        return east_vel - jnp.roll(east_vel, 1, 2) + (north_vel - dn_north) + (upward_vel - dn_up)

    divergence = jnp.concatenate(
        [divergence_of(star_pre, 0, len_pre), divergence_of(star_farm, len_pre, modes)], -1
    )
    mode_ids = jnp.arange(modes, dtype=jnp.int32)
    forward_x = hartley_x(mode_ids, mode_ids, len_pre, len_farm, False)
    spectral = jnp.einsum("zyx,mx->zmy", divergence, forward_x, precision=highest)
    cas_y = cas_square(total_y)
    dct_fwd, dct_inv = dct_tables(total_z)
    per_dev = modes // (count_z * count_y)
    pencil = lax.all_to_all(
        lax.all_to_all(spectral, "gz", split_axis=1, concat_axis=0, tiled=True),
        "gy",
        split_axis=1,
        concat_axis=2,
        tiled=True,
    )
    kx_modes = zone_z * (modes // count_z) + zone_y * per_dev + jnp.arange(per_dev, dtype=jnp.int32)
    ky_waves = jnp.arange(total_y, dtype=jnp.int32)
    wave_form = jnp.einsum("zjy,yk->zjk", pencil, cas_y, precision=highest)
    levels = jnp.einsum("mz,zjk->mjk", dct_fwd, wave_form, precision=highest)
    solved = solve_modes(levels, kx_modes, ky_waves, len_pre, len_farm, total_y)
    column_back = jnp.einsum("zm,mjk->zjk", dct_inv, solved, precision=highest)
    span_back = jnp.einsum("zjk,ky->zjy", column_back, cas_y / total_y, precision=highest)
    returned = lax.all_to_all(
        lax.all_to_all(span_back, "gz", split_axis=0, concat_axis=1, tiled=True),
        "gy",
        split_axis=2,
        concat_axis=1,
        tiled=True,
    )
    outer_block = mode_ids // (count_z * per_dev)
    inner_block = mode_ids % (count_z * per_dev) // per_dev
    remainder = mode_ids % per_dev
    row_modes = inner_block * (modes // count_z) + outer_block * per_dev + remainder
    inverse_x = hartley_x(row_modes, mode_ids, len_pre, len_farm, True)
    pressure = jnp.einsum("zpy,px->zyx", returned, inverse_x, precision=highest)
    high_north = span_neighbor(pressure[:, :1], -1)
    high_up = vertical_neighbor(pressure[:1], -1)

    def correct(star, first_col, last_col):
        press_part = pressure[..., first_col:last_col]
        step_x = jnp.roll(press_part, -1, 2) - press_part
        step_y = (
            jnp.concatenate([press_part[:, 1:], high_north[..., first_col:last_col]], 1)
            - press_part
        )
        step_z = (
            jnp.concatenate([press_part[1:], high_up[..., first_col:last_col]], 0) - press_part
        ) * below_top[:, None, None]
        return star - jnp.stack([step_x, step_y, step_z])

    return (correct(star_pre, 0, len_pre), correct(star_farm, len_pre, modes))


def solution(mesh):
    in_specs = (P(None, "gz", "gy", None), P(None, "gz", "gy", None), P(), P(), P("gy"))
    out_specs = (P(None, "gz", "gy", None), P(None, "gz", "gy", None))
    return jax.shard_map(body, mesh=mesh, in_specs=in_specs, out_specs=out_specs, check_vma=False)
```

profile of v0, /device:TPU:0, one launch (start us, length us, event | category | flops | bytes accessed | tf_op | source)
XLA Modules:
  0.0 2594.0 jit_solution(15804350732655567993)
XLA Ops:
  22.6 35.7 %fusion.207 = (f32[3,47,128,384]{3,2,1,0:T(8,128)}, f32[3,47,128,384]{3,2,1,0:T(8,128)}) fusion(f32[3,48,128,384]{3,2,1,0:T(8,128)} %param.8), kind=kLoop, calls=%fused_computation.339 | loop fusion | bytes 110886912 | tf_op jit(solution)/shard_map/slice | solution.py:126
  58.3 38.0 %fusion.206 = (f32[3,48,127,384]{3,2,1,0:T(8,128)}, f32[3,48,127,384]{3,2,1,0:T(8,128)}) fusion(f32[3,48,128,384]{3,2,1,0:T(8,128)} %param.8), kind=kLoop, calls=%fused_computation.338 | loop fusion | bytes 112361472 | tf_op jit(solution)/shard_map/slice | solution.py:124
  96.4 39.0 %fusion.204 = (f32[3,48,128,383]{3,2,1,0:T(8,128)}, f32[3,48,128,383]{3,2,1,0:T(8,128)}) fusion(f32[3,48,128,384]{3,2,1,0:T(8,128)} %param.8), kind=kLoop, calls=%fused_computation.336 | loop fusion | bytes 112951296 | tf_op jit(solution)/shard_map/jit(_roll_static)/slice | solution.py:129
  135.3 14.2 fusion.205
  149.6 23.4 fusion.203
  173.0 8.5 fusion.212
  182.1 8.4 fusion.213
  198.3 8.4 fusion.211
  212.7 11.2 reshape_squeeze.7
  224.8 9.2 copy.228
  237.6 321.1 %all-gather = f32[3,48,1024,1]{3,1,2,0:T(8,128)} all-gather(f32[3,48,128,1]{3,1,2,0:T(8,128)S(1)} %copy.228), channel_id=2, replica_groups=mesh['gz'=4,'gy'=8] {'gy'}, dimensions={2}, use_global_device_ids=true | all-gather | bytes 663552 | tf_op jit(solution)/shard_map/all_gather | solution.py:152
  558.7 43.1 %copy.168 = f32[3,48,1024,1]{2,1,0,3:T(8,128)S(1)} copy(f32[3,48,1024,1]{3,1,2,0:T(8,128)} %all-gather) | data formatting | bytes 1179648 | tf_op jit(solution)/shard_map/all_gather | solution.py:152
  604.7 12.7 copy.225
  617.4 9.0 copy.226
  626.4 9.2 copy.221
  635.7 9.0 copy.224
  644.7 13.3 copy.227
  658.1 9.1 copy.229
  667.2 13.0 copy.230
  690.6 21.0 gather_fusion
  711.7 18.3 broadcast_multiply_fusion
  730.0 33.7 %fusion.5 = f32[3,48,128,384]{3,2,1,0:T(8,128)} fusion(f32[3,48,128,383]{3,2,1,0:T(8,128)} %get-tuple-element.20, f32[3,48,128,1]{3,2,1,0:T(8,128)} %get-tuple-element.22, f32[3,48,128,1]{3,2,1,0:T(8,128)S(1)} %bitcast.154, f32[3,48,128,383]{3,2,1,0:T(8,128)} %get-tuple-element.19), kind=kLoop, calls=%fused_computation.18 | loop fusion | flops 28311552 | bytes 84934656 | tf_op jit(solution)/shard_map/mul | solution.py:28
  767.2 28.6 %fusion.3 = f32[3,48,128,384]{3,2,1,0:T(8,128)} fusion(f32[3,48,127,384]{3,2,1,0:T(8,128)} %get-tuple-element.24, f32[3,48,1,384]{3,2,1,0:T(1,128)S(1)} %copy.165, f32[3,48,1,384]{3,2,1,0:T(1,128)S(1)} %copy.164, f32[3,48,127,384]{3,2,1,0:T(8,128)} %get-tuple-element.23), kind=kLoop, calls=%fused_computation.16 | loop fusion | flops 28311552 | bytes 84934656 | tf_op jit(solution)/shard_map/mul | solution.py:29
  797.7 10.9 fusion.37
  811.6 28.1 %fusion.1 = f32[3,48,128,384]{3,2,1,0:T(8,128)} fusion(f32[3,47,128,384]{3,2,1,0:T(8,128)} %get-tuple-element.26, f32[3,1,128,384]{3,2,1,0:T(8,128)S(1)} %copy.167, f32[3,1,128,384]{3,2,1,0:T(8,128)S(1)} %copy.166, f32[3,47,128,384]{3,2,1,0:T(8,128)} %get-tuple-element.25), kind=kLoop, calls=%fused_computation.14 | loop fusion | flops 28311552 | bytes 84934656 | tf_op jit(solution)/shard_map/mul | solution.py:30
  839.7 32.8 %fusion.23 = f32[48,128,384]{2,1,0:T(8,128)} fusion(f32[3,48,128,384]{3,2,1,0:T(8,128)} %fusion.3, f32[3,48,128,384]{3,2,1,0:T(8,128)} %fusion.1, f32[3,48,128,384]{3,2,1,0:T(8,128)} %fusion.5), kind=kLoop, calls=%fused_computation.43 | loop fusion | flops 40108032 | bytes 94371840 | tf_op jit(solution)/shard_map/mul | solution.py:38
  872.5 87.0 %multiply_add_fusion = f32[3,48,128,384]{3,2,1,0:T(8,128)} fusion(f32[3,48,128,384]{3,2,1,0:T(8,128)} %param.8, f32[3,47,128,384]{3,2,1,0:T(8,128)} %get-tuple-element.26, f32[3,1,128,384]{3,2,1,0:T(8,128)S(1)} %copy.167, f32[3,1,128,384]{3,2,1,0:T(8,128)S(1)} %copy.166, f32[3,47,128,384]{3,2,1,0:T(8,128)} %get-tuple-element.25, ...), kind=kLoop, calls=%fused_computation.12 | loop fusion | flops 176947200 | bytes 264241152 | tf_op jit(solution)/shard_map/add | solution.py:38
  959.5 8.6 slice.495
  968.0 12.7 slice.496
  980.7 10.7 reshape_squeeze.6
  991.4 11.6 scatter_fusion
  1003.0 11.5 broadcast_in_dim_reshape.3
  1014.5 12.8 add_multiply_fusion
  1027.4 9.9 copy-done.1
  1053.3 36.8 %add_multiply_fusion.1 = f32[3,48,128,128]{3,1,2,0:T(8,128)} fusion(f32[3,48,127,128]{3,1,2,0:T(8,128)} %copy.221, f32[3,48,1,128]{3,1,2,0:T(8,128)S(1)} %copy-done.16, f32[3,48,1,128]{3,1,2,0:T(8,128)S(1)} %copy-done.14, f32[3,48,127,128]{3,1,2,0:T(8,128)} %copy.224, f32[3,47,128,128]{3,1,2,0:T(8,128)} %copy.225, f32[3,1,128,128]{3,1,2,0:T(1,128)S(1)} %slice.468, ...), kind=kLoop, calls=%fused_computation.76 | loop fusion | flops 61341696 | bytes 88080960 | tf_op jit(solution)/shard_map/mul | solution.py:163
  1097.9 11.3 slice_bitcast_fusion.1
  1109.2 11.6 slice_bitcast_fusion.3
  1134.2 23.2 fusion.17
  1157.4 10.9 fusion.235
  1168.3 55.8 %fusion.46 = f32[48,512,128]{2,1,0:T(8,128)} fusion(s32[512]{0:T(512)S(1)} %bitcast.186, f32[512]{0:T(512)S(1)} %copy-done.30, s32[512]{0:T(512)S(1)} %copy-done.22, pred[512]{0:T(512)(128)(4,1)S(1)} %copy-done.32, f32[48,128,512]{2,1,0:T(8,128)} %fusion.235), kind=kOutput, calls=%fused_computation.92 | convolution fusion | flops 19330760704 | bytes 25172480 | tf_op jit(solution)/shard_map/zyx,mx->zmy/dot_general | solution.py:179
  1224.1 16.6 copy.176
  1240.8 285.0 %all_to_all.72 = f32[48,512,128]{2,0,1:T(8,128)} all-to-all(f32[48,512,128]{2,0,1:T(8,128)} %copy.176), channel_id=1, replica_groups=mesh['gz'=4,'gy'=8] {'gz'}, dimensions={1} | all-to-all | bytes 25165824 | tf_op jit(solution)/shard_map/all_to_all | solution.py:184
  1525.8 13.2 copy.178
  1539.0 16.5 copy.179
  1561.6 17.5 fusion.231
  1579.1 17.7 fusion.233
  1596.8 103.0 %all-to-all-done.1 = f32[192,128,128]{2,0,1:T(8,128)} async-done(((f32[192,128,128]{2,0,1:T(8,128)}), f32[192,128,128]{2,0,1:T(8,128)}, u32[]{:S(2)}, u32[]{:S(2)}) %all-to-all-start.1) | async-done | bytes 12582944 | tf_op jit(solution)/shard_map/all_to_all | solution.py:183
  1699.8 16.6 copy.233
  1716.4 13.6 all_to_all.59
  1730.1 52.6 %fusion.11 = f32[192,16,1024]{2,0,1:T(8,128)} fusion(f32[192,16,1024]{2,1,0:T(8,128)} %all_to_all.59, f32[1024,1024,1]{1,0,2:T(8,128)} %fusion.231), kind=kOutput, calls=%fused_computation.26 | convolution fusion | flops 38654705664 | bytes 29360128 | tf_op jit(solution)/shard_map/zjy,yk->zjk/dot_general | solution.py:192
  1782.7 19.1 fusion.137
  1801.8 18.3 fusion.15
  1820.1 51.3 %fusion.13 = f32[192,16,1024]{2,1,0:T(8,128)S(1)} fusion(f32[192,16,1024]{2,0,1:T(8,128)} %fusion.15, f32[1024,1024,1]{1,0,2:T(8,128)S(1)} %copy-done.10), kind=kOutput, calls=%fused_computation.28 | convolution fusion | flops 38654705664 | bytes 29360128 | tf_op jit(solution)/shard_map/zjk,ky->zjy/dot_general | solution.py:196
  1871.4 274.1 %all_to_all.73 = f32[192,16,1024]{2,1,0:T(8,128)} all-to-all(f32[192,16,1024]{2,1,0:T(8,128)S(1)} %fusion.13), channel_id=1, replica_groups=mesh['gz'=4,'gy'=8] {'gz'}, dimensions={0} | all-to-all | bytes 25165824 | tf_op jit(solution)/shard_map/all_to_all | solution.py:198
  2145.5 11.9 copy.183
  2157.4 20.9 copy.184
  2178.4 20.5 reshape.505
  2204.3 138.9 %all-to-all-done.3 = f32[8,1,393216]{2,1,0:T(1,128)} async-done(((f32[8,1,393216]{2,1,0:T(1,128)}), f32[8,1,393216]{2,1,0:T(1,128)}, u32[]{:S(2)}, u32[]{:S(2)}) %all-to-all-start.3) | async-done | bytes 12582944 | tf_op jit(solution)/shard_map/all_to_all | solution.py:197
  2343.8 36.7 %reduce = f32[8,393216]{1,0:T(8,128)} reduce(f32[8,1,393216]{2,1,0:T(1,128)} %all-to-all-done.3, f32[]{:T(128)} %broadcast.1061), dimensions={1}, to_apply=%all_to_all.64.reduce_sub_computation | reduce | bytes 25165828 | tf_op jit(solution)/shard_map/all_to_all | solution.py:197
  2380.5 23.2 reshape.506
  2403.7 18.7 copy.186
  2422.4 73.3 %fusion.85 = f32[48,128,512]{2,1,0:T(8,128)S(1)} fusion(f32[48,512,128]{2,1,0:T(8,128)} %bitcast.162, s32[512]{0:T(512)S(1)} %bitcast.187, f32[512]{0:T(512)S(1)} %get-tuple-element.59, s32[512]{0:T(512)S(1)} %get-tuple-element.58, s32[512]{0:T(512)S(1)} %copy-done.23, pred[512]{0:T(512)(128)(4,1)S(1)} %copy-done.33, ...), kind=kOutput, calls=%fused_computation.150 | convolution fusion | flops 19331022848 | bytes 25175040 | tf_op jit(solution)/shard_map/zpy,px->zyx/dot_general | solution.py:209
  2541.0 26.0 %fusion.32 = (f32[1,48,128,384]{3,2,1,0:T(8,128)}, f32[1,48,128,384]{3,2,1,0:T(8,128)}, f32[1,48,128,384]{3,2,1,0:T(8,128)}) fusion(f32[48,128,1]{2,1,0:T(8,128)} %get-tuple-element.34, f32[48,128,383]{2,1,0:T(8,128)} %slice.523, f32[48,128,512]{2,1,0:T(8,128)} %copy-done, f32[48,1,384]{2,1,0:T(1,128)S(1)} %slice-done.31, f32[48,127,384]{2,1,0:T(8,128)} %slice.526, ...), kind=kLoop, calls=%fused_computation.67 | loop fusion | flops 16515072 | bytes 66060480 | tf_op jit(solution)/shard_map/stack | solution.py:223
  2567.1 26.8 %maximum_subtract_fusion = f32[3,48,128,384]{3,2,1,0:T(8,128)} fusion(f32[1,48,128,384]{3,2,1,0:T(8,128)} %get-tuple-element.33, f32[1,48,128,384]{3,2,1,0:T(8,128)} %get-tuple-element.32, f32[1,48,128,384]{3,2,1,0:T(8,128)} %get-tuple-element.31, f32[3,48]{1,0:T(4,128)S(1)} %copy-done.21, f32[3,48,128]{2,1,0:T(8,128)S(1)} %copy-done.12, ...), kind=kLoop, calls=%fused_computation.10 | loop fusion | flops 56623104 | bytes 85010496 | tf_op jit(solution)/shard_map/sub | solution.py:223
  (271 shorter events, 156.3 us)
Async XLA Ops:
  5.3 803.3 %collective-permute-start.2 = (f32[3,1,128,512]{3,1,2,0:T(1,128)}, f32[3,1,128,512]{3,1,2,0:T(1,128)}, u32[]{:S(2)}, u32[]{:S(2)}) collective-permute-start(f32[3,1,128,512]{3,1,2,0:T(1,128)} %pad_maximum_fusion.13), channel_id=1, source_target_pairs={{8,0},{16,8},{24,16},{9,1},{17,9},{25,17},{10,2},{18,10},{26,18},{... | collective-permute-start | bytes 2359304 | tf_op jit(solution)/shard_map/ppermute | solution.py:24
  8.8 801.2 %collective-permute-start.3 = (f32[3,1,128,512]{3,1,2,0:T(1,128)}, f32[3,1,128,512]{3,1,2,0:T(1,128)}, u32[]{:S(2)}, u32[]{:S(2)}) collective-permute-start(f32[3,1,128,512]{3,1,2,0:T(1,128)} %pad_maximum_fusion.14), channel_id=1, source_target_pairs={{0,8},{8,16},{16,24},{1,9},{9,17},{17,25},{2,10},{10,18},{18,26},{... | collective-permute-start | bytes 2359304 | tf_op jit(solution)/shard_map/ppermute | solution.py:24
  19.8 745.1 %collective-permute-start = (f32[3,48,1,512]{3,1,2,0:T(8,128)}, f32[3,48,1,512]{3,1,2,0:T(8,128)}, u32[]{:S(2)}, u32[]{:S(2)}) collective-permute-start(f32[3,48,1,512]{3,1,2,0:T(8,128)} %pad_maximum_fusion.15), channel_id=1, source_target_pairs={{1,0},{2,1},{3,2},{4,3},{5,4},{6,5},{7,6},{0,7},{9,8},{10,9},{11,1... | collective-permute-start | bytes 884744 | tf_op jit(solution)/shard_map/ppermute | solution.py:18
  22.3 743.7 %collective-permute-start.1 = (f32[3,48,1,512]{3,1,2,0:T(8,128)}, f32[3,48,1,512]{3,1,2,0:T(8,128)}, u32[]{:S(2)}, u32[]{:S(2)}) collective-permute-start(f32[3,48,1,512]{3,1,2,0:T(8,128)} %pad_maximum_fusion.16), channel_id=1, source_target_pairs={{7,0},{0,1},{1,2},{2,3},{3,4},{4,5},{5,6},{6,7},{15,8},{8,9},{9,10... | collective-permute-start | bytes 884744 | tf_op jit(solution)/shard_map/ppermute | solution.py:18
  135.3 37.6 %slice-start = ((s8[9437184]{0:T(1024)(128)(4,1)}), s8[4194304]{0:T(1024)(128)(4,1)S(1)}, s32[]{:S(2)}) async-start(s8[9437184]{0:T(1024)(128)(4,1)} %bitcast.145), calls=%async_computation.4 | async-start | bytes 8388608
  135.3 37.6 %slice-start.1 = ((s8[9437184]{0:T(1024)(128)(4,1)}), s8[4194304]{0:T(1024)(128)(4,1)S(1)}, s32[]{:S(2)}) async-start(s8[9437184]{0:T(1024)(128)(4,1)} %bitcast.145), calls=%async_computation.5 | async-start | bytes 8388608
  149.6 23.4 slice-start.2
  173.0 8.5 copy-start.34
  212.7 11.3 copy-start.35
  604.7 12.7 slice-start.28
  604.7 12.7 slice-start.29
  604.7 12.7 slice-start.30
  617.3 9.1 slice-start.19
  617.4 9.0 slice-start.20
  617.4 9.0 slice-start.21
  626.4 9.3 slice-start.16
  626.4 9.3 slice-start.17
  626.4 9.3 slice-start.18
  635.7 22.3 slice-start.25
  635.7 22.3 slice-start.26
  644.7 13.3 slice-start.27
  667.2 13.0 copy-start.7
  667.2 16.5 copy-start.6
  680.2 6.9 copy-start.5
  687.1 42.9 %slice-start.10 = ((s8[9437184]{0:T(1024)(128)(4,1)}), s8[1048576]{0:T(1024)(128)(4,1)S(1)}, s32[]{:S(2)}) async-start(s8[9437184]{0:T(1024)(128)(4,1)} %bitcast.153), calls=%async_computation.14 | async-start | bytes 2097152
  711.6 18.4 slice-start.11
  711.6 18.4 slice-start.12
  796.8 14.9 copy-start.13
  797.7 13.9 copy-start.15
  980.7 10.7 copy-start.27
  980.7 10.7 copy-start.29
  1003.0 11.5 copy-start.11
  1003.0 11.5 copy-start.20
  1003.0 11.5 copy-start.24
  1014.5 32.6 %slice-start.22 = ((s8[9437184]{0:T(1024)(128)(4,1)}), s8[1048576]{0:T(1024)(128)(4,1)S(1)}, s32[]{:S(2)}) async-start(s8[9437184]{0:T(1024)(128)(4,1)} %bitcast.168), calls=%async_computation.26 | async-start | bytes 2097152
  1014.5 32.6 %slice-start.23 = ((s8[9437184]{0:T(1024)(128)(4,1)}), s8[4194304]{0:T(1024)(128)(4,1)S(1)}, s32[]{:S(2)}) async-start(s8[9437184]{0:T(1024)(128)(4,1)} %bitcast.168), calls=%async_computation.27 | async-start | bytes 8388608
  1027.4 10.0 copy-start.1
  1038.3 8.8 slice-start.24
  1097.9 25.7 slice-start.4
  1097.9 25.7 slice-start.5
  1109.2 17.4 copy-start.3
  1109.2 14.4 slice-start.6
  1121.3 8.0 collective-permute-start.5
  1123.0 6.2 collective-permute-start.4
  1157.4 10.9 copy-start.22
  1157.4 10.9 copy-start.30
  1157.4 10.9 copy-start.31
  1157.4 10.9 copy-start.32
  1555.4 144.3 %all-to-all-start.1 = ((f32[192,128,128]{2,0,1:T(8,128)}), f32[192,128,128]{2,0,1:T(8,128)}, u32[]{:S(2)}, u32[]{:S(2)}) async-start(f32[192,128,128]{2,0,1:T(8,128)} %copy.179), calls=%async_computation.1 | async-start | bytes 25165824 | tf_op jit(solution)/shard_map/all_to_all | solution.py:183
  1801.8 18.3 copy-start.10
  2198.9 144.3 %all-to-all-start.3 = ((f32[8,1,393216]{2,1,0:T(1,128)}), f32[8,1,393216]{2,1,0:T(1,128)}, u32[]{:S(2)}, u32[]{:S(2)}) async-start(f32[8,1,393216]{2,1,0:T(1,128)} %reshape.505), calls=%async_computation.3 | async-start | bytes 25165824 | tf_op jit(solution)/shard_map/all_to_all | solution.py:197
  2403.7 18.7 copy-start.23
  2403.7 18.7 copy-start.33
  2495.7 22.3 copy-start
  2495.8 31.4 %collective-permute-start.7 = (f32[1,128,512]{2,1,0:T(8,128)S(1)}, f32[1,128,512]{2,1,0:T(8,128)S(1)}, u32[]{:S(2)}, u32[]{:S(2)}) collective-permute-start(f32[1,128,512]{2,1,0:T(8,128)S(1)} %slice.521), channel_id=1, source_target_pairs={{8,0},{16,8},{24,16},{9,1},{17,9},{25,17},{10,2},{18,10},{26,18},{... | collective-permute-start | bytes 786440 | tf_op jit(solution)/shard_map/ppermute | solution.py:24
  2497.1 30.0 %collective-permute-start.6 = (f32[48,1,512]{2,1,0:T(1,128)S(1)}, f32[48,1,512]{2,1,0:T(1,128)S(1)}, u32[]{:S(2)}, u32[]{:S(2)}) collective-permute-start(f32[48,1,512]{2,1,0:T(1,128)S(1)} %slice.518), channel_id=1, source_target_pairs={{1,0},{2,1},{3,2},{4,3},{5,4},{6,5},{7,6},{0,7},{9,8},{10,9},{11,1... | collective-permute-start | bytes 294920 | tf_op jit(solution)/shard_map/ppermute | solution.py:18
  2519.8 8.1 slice-start.3
  2525.3 7.7 slice-start.7
  2534.3 32.7 %slice-start.13 = ((s8[9437184]{0:T(1024)(128)(4,1)}), s8[4194304]{0:T(1024)(128)(4,1)S(1)}, s32[]{:S(2)}) async-start(s8[9437184]{0:T(1024)(128)(4,1)} %bitcast.155), calls=%async_computation.17 | async-start | bytes 8388608
  2540.9 26.1 %slice-start.14 = ((s8[9437184]{0:T(1024)(128)(4,1)}), s8[4194304]{0:T(1024)(128)(4,1)S(1)}, s32[]{:S(2)}) async-start(s8[9437184]{0:T(1024)(128)(4,1)} %bitcast.155), calls=%async_computation.18 | async-start | bytes 8388608
  2540.9 26.1 %slice-start.15 = ((s8[9437184]{0:T(1024)(128)(4,1)}), s8[1048576]{0:T(1024)(128)(4,1)S(1)}, s32[]{:S(2)}) async-start(s8[9437184]{0:T(1024)(128)(4,1)} %bitcast.155), calls=%async_computation.19 | async-start | bytes 2097152
  2540.9 26.1 %copy-start.12 = (f32[3,48,128]{2,1,0:T(8,128)S(1)}, f32[3,48,128]{2,1,0:T(8,128)}, u32[]{:S(2)}) copy-start(f32[3,48,128]{2,1,0:T(8,128)} %copy.170) | copy-start | bytes 221188
  2540.9 26.1 %copy-start.21 = (f32[3,48]{1,0:T(4,128)S(1)}, f32[3,48]{1,0:T(4,128)}, u32[]{:S(2)}) copy-start(f32[3,48]{1,0:T(4,128)} %pad_convert_fusion) | copy-start | bytes 1732
  2541.0 26.1 %copy-start.25 = (f32[384]{0:T(512)S(1)}, f32[384]{0:T(512)}, u32[]{:S(2)}) copy-start(f32[384]{0:T(512)} %convert_multiply_fusion) | copy-start | bytes 4612
  (14 other events, 63.5 us)
where the time goes:
time: 2600 us; the launch traced here: 2590 us
  blocking collectives  880 us (34%)
  local copies, waits for them, and re-layouts  655 us (25%)
  other arithmetic  520 us (20%)
  matrix products  270 us (10%)
  waiting for transfers between devices  242 us (9%)
    all_gather x1, blocking collectives, body(): whole_plane = lax.all_gather(outlet, 'gy', axis=2, tiled=True)  321 us
    all_to_all x1, blocking collectives, body(): lax.all_to_all(spectral, 'gz', split_axis=1, concat_axis=0, tiled=True)  285 us
    all_to_all x1, blocking collectives, body(): lax.all_to_all(span_back, 'gz', split_axis=0, concat_axis=1, tiled=True)  274 us
    unnamed x152, local copies, waits for them, and re-layouts  159 us
    all_to_all x1, waiting for transfers between devices, body(): lax.all_to_all(lax.all_to_all(span_back, 'gz', split_axis=0, concat_axis=...  139 us
    all_to_all x1, waiting for transfers between devices, body(): lax.all_to_all(lax.all_to_all(spectral, 'gz', split_axis=1, concat_axis=0...  103 us
    add x1, other arithmetic, tendency(): return velocity + time_step * (eddy_visc * laplace - advect)  87 us
    dot_general x1, matrix products, body(): pressure = jnp.einsum('zpy,px->zyx', returned, inverse_x, precision=highest)  73.3 us
  transfers between devices with their start and end apart: 10, of which 2 were waited for; matrix products, arithmetic and copies ran while one was open for 21% of the time, Pallas kernels for 0%

commit v1 on v0

--- a/solution.py
+++ b/solution.py
@@ -1,6 +1,10 @@
+import functools
+
 import jax
 import jax.numpy as jnp
 from jax import lax
+from jax.experimental import pallas as pl
+from jax.experimental.pallas import tpu as pltpu
 from jax.sharding import PartitionSpec as P
 
 FRINGE = 32
@@ -46,6 +50,11 @@
     return shifted_2(planes, "gz", offset)
 
 
+def eigen(wavenum, length):
+    sine_val = jnp.sin(jnp.pi * wavenum.astype(jnp.float32) / length)
+    return 4.0 * sine_val * sine_val
+
+
 def dct_tables(count):
     integer_ids = jnp.arange(count, dtype=jnp.int32)
     phases = integer_ids[:, None] * (2 * integer_ids[None, :] + 1) % (4 * count)
@@ -55,52 +64,123 @@
     return (forward, inverse)
 
 
-def cas_square(count):
-    integer_ids = jnp.arange(count, dtype=jnp.int32)
-    phases = integer_ids[:, None] * integer_ids[None, :] % count
-    angles = 2.0 * jnp.pi * phases.astype(jnp.float32) / count
+def hartley(count):
+    ids = jnp.arange(count, dtype=jnp.int32)
+    angles = 2.0 * jnp.pi * (ids[:, None] * ids[None, :] % count).astype(jnp.float32) / count
     return jnp.cos(angles) + jnp.sin(angles)
 
 
-def hartley_x(mode_ids, cell_ids, len_pre, len_farm, inverse):
-    mode_farm = mode_ids >= len_pre
-    cell_farm = cell_ids >= len_pre
-    wavenum = jnp.where(mode_farm, mode_ids - len_pre, mode_ids)
-    places = jnp.where(cell_farm, cell_ids - len_pre, cell_ids)
-    length = jnp.where(mode_farm, len_farm, len_pre)
-    phases = wavenum[:, None] * places[None, :] % length[:, None]
-    angles = 2.0 * jnp.pi * phases.astype(jnp.float32) / length[:, None].astype(jnp.float32)
-    same_domain = (mode_farm[:, None] == cell_farm[None, :]).astype(jnp.float32)
-    matrix = (jnp.cos(angles) + jnp.sin(angles)) * same_domain
-    if inverse:
-        matrix = matrix / length[:, None].astype(jnp.float32)
-    return matrix
-
-
-def eigen(wavenum, length):
-    sine_val = jnp.sin(jnp.pi * wavenum.astype(jnp.float32) / length)
-    return 4.0 * sine_val * sine_val
-
-
-def solve_modes(spectrum, kx_modes, ky_waves, len_pre, len_farm, total_y):
-    depth_all = spectrum.shape[0]
-    wave_z = jnp.arange(depth_all, dtype=jnp.int32)
-    mode_farm = kx_modes >= len_pre
-    wavenum = jnp.where(mode_farm, kx_modes - len_pre, kx_modes)
-    length = jnp.where(mode_farm, len_farm, len_pre).astype(jnp.float32)
-    sine_val = jnp.sin(jnp.pi * wavenum.astype(jnp.float32) / length)
-    rate_x = 4.0 * sine_val * sine_val
-    summed = (
-        eigen(wave_z, 2 * depth_all)[:, None, None]
-        + rate_x[None, :, None]
-        + eigen(ky_waves, total_y)[None, None, :]
-    )
-    null_mode = (
-        (wave_z[:, None, None] == 0)
-        & (wavenum[None, :, None] == 0)
-        & (ky_waves[None, None, :] == 0)
-    )
-    return jnp.where(null_mode, 0.0, -spectrum / jnp.where(null_mode, 1.0, summed))
+def sine_table(span):
+    ids = jnp.arange(span, dtype=jnp.int32)
+    phases = ids[:, None] * ids[None, :] % (2 * span)
+    table = jnp.sqrt(2.0 / span) * jnp.sin(jnp.pi * phases.astype(jnp.float32) / span)
+    return table.at[0, 0].set(1.0)
+
+
+def mm(a, b, dims=(((1,), (0,)), ((), ()))):
+    return lax.dot_general(a, b, dims, precision=highest, preferred_element_type=jnp.float32)
+
+
+def forward_kernel(block, rate_ref, r_ref, dct_ref, dst_ref, base_ref, edge_ref, g_ref, e_ref):
+    first = pl.program_id(0) * block
+    parts, _, depth, span = r_ref.shape
+    lane = lax.broadcasted_iota(jnp.int32, base_ref.shape, 1)
+
+    def step(k, carry):
+        column = r_ref[:, k].reshape(parts * depth, span)
+        modal = mm(mm(dct_ref[...], column), dst_ref[...])
+        scale = jnp.where(lane == 0, 1.0, base_ref[...] + rate_ref[first + k])
+        solved = -modal / scale
+        g_ref[k] = solved
+        e_ref[k] = mm(edge_ref[...], solved, (((1,), (1,)), ((), ())))
+        return carry
+
+    lax.fori_loop(0, block, step, 0)
+
+
+def backward_kernel(block, rate_ref, g_ref, p_ref, dct_ref, dst_ref, base_ref, edge_ref, o_ref):
+    first = pl.program_id(0) * block
+    parts, _, depth, span = o_ref.shape
+    lane = lax.broadcasted_iota(jnp.int32, base_ref.shape, 1)
+
+    def step(k, carry):
+        border = mm(p_ref[k], edge_ref[...], (((0,), (0,)), ((), ())))
+        scale = base_ref[...] + rate_ref[first + k]
+        modal = jnp.where(lane == 0, border, g_ref[k] + border / scale)
+        column = mm(dct_ref[...], mm(modal, dst_ref[...]))
+        o_ref[:, k] = column.reshape(parts, depth, span)
+        return carry
+
+    lax.fori_loop(0, block, step, 0)
+
+
+def solve_pressure(spectral, rate_x, count_z, count_y, zone_y, total_z):
+    modes, depth, span = spectral.shape
+    per = modes // count_z
+    block = 8
+    whole = lax.all_to_all(spectral, "gz", split_axis=0, concat_axis=0, tiled=True)
+    whole = whole.reshape(count_z, per, depth, span)
+    dct_fwd, dct_inv = dct_tables(total_z)
+    dst = sine_table(span)
+    ids = jnp.arange(span, dtype=jnp.int32)
+    rate_z = eigen(jnp.arange(total_z, dtype=jnp.int32), 2 * total_z)
+    rate_y = jnp.where(ids == 0, 1.0, eigen(ids, 2 * span))
+    base = rate_z[:, None] + rate_y[None, :]
+    tail = dst[span - 1]
+    lead = jnp.where(ids == 0, 1.0, dst[1])
+    edge = jnp.zeros((8, span), jnp.float32).at[0].set(lead).at[1].set(tail)
+    full = lambda *shape: pl.BlockSpec(shape, lambda i: (0,) * len(shape))
+    smem = pl.BlockSpec(memory_space=pltpu.SMEM)
+    columns = pl.BlockSpec((count_z, block, depth, span), lambda i: (0, i, 0, 0))
+    modal = pl.BlockSpec((block, total_z, span), lambda i: (i, 0, 0))
+    pairs = pl.BlockSpec((block, 8, total_z), lambda i: (i, 0, 0))
+    params = pltpu.CompilerParams(vmem_limit_bytes=48 << 20)
+    solved, ends = pl.pallas_call(
+        functools.partial(forward_kernel, block),
+        grid=(per // block,),
+        in_specs=[smem, columns, full(total_z, total_z), full(span, span), full(total_z, span), full(8, span)],
+        out_specs=[modal, pairs],
+        out_shape=[
+            jax.ShapeDtypeStruct((per, total_z, span), jnp.float32),
+            jax.ShapeDtypeStruct((per, 8, total_z), jnp.float32),
+        ],
+        compiler_params=params,
+        name="solve_forward",
+    )(rate_x, whole, dct_fwd, dst, base, edge)
+    sent = jnp.concatenate([ends[:, 0], ends[:, 1]], 0)
+    every = lax.all_gather(sent, "gy", axis=0)
+    given = every[:, :per] + jnp.roll(every[:, per:], 1, 0)
+    cas = hartley(count_y)
+    rate = rate_x[:, None] + rate_z[None, :]
+    null = rate == 0.0
+    safe = jnp.where(null, 1.0, rate)
+    half = 0.5 * jnp.sqrt(safe)
+    root = jnp.sqrt(1.0 + half * half)
+    theta = 2.0 * jnp.log1p(half + half * half / (1.0 + root))
+    decay = jnp.exp(-span * theta)
+    lift = -jnp.expm1(-span * theta)
+    turn = 0.5 * eigen(jnp.arange(count_y, dtype=jnp.int32), count_y)[:, None, None]
+    factor = (4.0 * half * root) / (lift * (1.0 + decay))
+    symbol = factor * (lift * lift + 2.0 * decay * turn)
+    symbol = jnp.where(null, 2.0 * turn / span, symbol)
+    drop = symbol == 0.0
+    inner = jnp.einsum("kj,jxm->kxm", cas, given, precision=highest)
+    inner = jnp.where(drop, 0.0, inner / jnp.where(drop, 1.0, symbol)) / count_y
+    own = jnp.stack([zone_y, (zone_y + 1) % count_y])
+    rows = jnp.sum(jnp.where(own[:, None, None] == jnp.arange(count_y)[None, :, None], cas[None], 0.0), 1)
+    borders = jnp.einsum("ik,kxm->xim", rows, inner, precision=highest)
+    borders = jnp.concatenate([borders, jnp.zeros((per, 6, total_z), jnp.float32)], 1)
+    back = pl.pallas_call(
+        functools.partial(backward_kernel, block),
+        grid=(per // block,),
+        in_specs=[smem, modal, pairs, full(total_z, total_z), full(span, span), full(total_z, span), full(8, span)],
+        out_specs=columns,
+        out_shape=jax.ShapeDtypeStruct((count_z, per, depth, span), jnp.float32),
+        compiler_params=params,
+        name="solve_backward",
+    )(rate_x, solved, borders, dct_inv, dst, base, edge)
+    back = back.reshape(modes, depth, span)
+    return lax.all_to_all(back, "gz", split_axis=0, concat_axis=0, tiled=True)
 
 
 def body(vel_pre, vel_farm, thrust, turbine_cells, inflow_rows):
@@ -148,9 +228,13 @@
         .reshape(depth, span, len_farm)
     )
     star_farm = jnp.concatenate([stream_new[None], star_farm[1:]], 0)
-    outlet = vel_pre[:, :, :, -1]
-    whole_plane = lax.all_gather(outlet, "gy", axis=2, tiled=True)
-    inflow = jnp.take(whole_plane, inflow_rows, axis=2)
+    outlet = vel_pre[:, :, :, -1].reshape(3 * depth, span)
+    whole_plane = lax.all_gather(outlet, "gy", axis=0)
+    chosen = (
+        inflow_rows[None, :, None]
+        == jnp.arange(total_y, dtype=jnp.int32).reshape(count_y, 1, span)
+    ).astype(jnp.float32)
+    inflow = jnp.einsum("gcs,gys->cy", whole_plane, chosen, precision=highest).reshape(3, depth, span)
     weight = (
         jnp.maximum(FRINGE - jnp.arange(len_farm, dtype=jnp.int32), 0).astype(jnp.float32) / FRINGE
     )
@@ -171,42 +255,27 @@
         dn_up = jnp.concatenate([low_up[..., first_col:last_col], upward_vel[:-1]], 0)
         return east_vel - jnp.roll(east_vel, 1, 2) + (north_vel - dn_north) + (upward_vel - dn_up)
 
-    divergence = jnp.concatenate(
-        [divergence_of(star_pre, 0, len_pre), divergence_of(star_farm, len_pre, modes)], -1
-    )
-    mode_ids = jnp.arange(modes, dtype=jnp.int32)
-    forward_x = hartley_x(mode_ids, mode_ids, len_pre, len_farm, False)
-    spectral = jnp.einsum("zyx,mx->zmy", divergence, forward_x, precision=highest)
-    cas_y = cas_square(total_y)
-    dct_fwd, dct_inv = dct_tables(total_z)
-    per_dev = modes // (count_z * count_y)
-    pencil = lax.all_to_all(
-        lax.all_to_all(spectral, "gz", split_axis=1, concat_axis=0, tiled=True),
-        "gy",
-        split_axis=1,
-        concat_axis=2,
-        tiled=True,
-    )
-    kx_modes = zone_z * (modes // count_z) + zone_y * per_dev + jnp.arange(per_dev, dtype=jnp.int32)
-    ky_waves = jnp.arange(total_y, dtype=jnp.int32)
-    wave_form = jnp.einsum("zjy,yk->zjk", pencil, cas_y, precision=highest)
-    levels = jnp.einsum("mz,zjk->mjk", dct_fwd, wave_form, precision=highest)
-    solved = solve_modes(levels, kx_modes, ky_waves, len_pre, len_farm, total_y)
-    column_back = jnp.einsum("zm,mjk->zjk", dct_inv, solved, precision=highest)
-    span_back = jnp.einsum("zjk,ky->zjy", column_back, cas_y / total_y, precision=highest)
-    returned = lax.all_to_all(
-        lax.all_to_all(span_back, "gz", split_axis=0, concat_axis=1, tiled=True),
-        "gy",
-        split_axis=2,
-        concat_axis=1,
-        tiled=True,
-    )
-    outer_block = mode_ids // (count_z * per_dev)
-    inner_block = mode_ids % (count_z * per_dev) // per_dev
-    remainder = mode_ids % per_dev
-    row_modes = inner_block * (modes // count_z) + outer_block * per_dev + remainder
-    inverse_x = hartley_x(row_modes, mode_ids, len_pre, len_farm, True)
-    pressure = jnp.einsum("zpy,px->zyx", returned, inverse_x, precision=highest)
+    cas_pre = hartley(len_pre)
+    cas_farm = hartley(len_farm)
+    spectral = jnp.concatenate(
+        [
+            jnp.einsum("mx,zyx->mzy", cas_pre, divergence_of(star_pre, 0, len_pre), precision=highest),
+            jnp.einsum("mx,zyx->mzy", cas_farm, divergence_of(star_farm, len_pre, modes), precision=highest),
+        ],
+        0,
+    )
+    kx_modes = zone_z * (modes // count_z) + jnp.arange(modes // count_z, dtype=jnp.int32)
+    rate_x = jnp.where(
+        kx_modes < len_pre, eigen(kx_modes, len_pre), eigen(kx_modes - len_pre, len_farm)
+    )
+    solved = solve_pressure(spectral, rate_x, count_z, count_y, zone_y, total_z)
+    pressure = jnp.concatenate(
+        [
+            jnp.einsum("mzy,mx->zyx", solved[:len_pre], cas_pre / len_pre, precision=highest),
+            jnp.einsum("mzy,mx->zyx", solved[len_pre:], cas_farm / len_farm, precision=highest),
+        ],
+        -1,
+    )
     high_north = span_neighbor(pressure[:, :1], -1)
     high_up = vertical_neighbor(pressure[:1], -1)
 

time: 2600 us -> 1970 us (0.76)
  blocking collectives: 880 us -> 290 us
  Pallas kernels: 0 us -> 252 us
  matrix products: 270 us -> 80.5 us
  local copies, waits for them, and re-layouts: 655 us -> 541 us
  other arithmetic: 520 us -> 466 us
  waiting for transfers between devices: 242 us -> 296 us
    all_gather x1, blocking collectives: 321 us -> 11.7 us  [body(): whole_plane = lax.all_gather(outlet, 'gy', axis=0)]
    all_to_all x2 -> x1, blocking collectives: 559 us -> 278 us  [solve_pressure(): return lax.all_to_all(back, 'gz', split_axis=0, concat_axis=0, tiled=True)]
    pallas_call x0 -> x2, Pallas kernels: none -> 252 us  [the longest x1 132 us: solve_pressure(): pl.pallas_call(functools.partial(forward_kernel, block), grid=(per // blo...]
    dot_general x6 -> x7, matrix products: 270 us -> 80.5 us  [the longest x1 35 us: body(): jnp.einsum('mx,zyx->mzy', cas_farm, divergence_of(star_farm, len_pre, mod...]
    all_to_all x8 -> x0, local copies, waits for them, and re-layouts: 112 us -> none  [the longest x2 32.9 us: body(): lax.all_to_all(span_back, 'gz', split_axis=0, concat_axis=1, tiled=True)]
    unnamed x152 -> x73, local copies, waits for them, and re-layouts: 159 us -> 90.1 us
    dot_general x3 -> x0, other arithmetic: 46.1 us -> none  [the longest x1 17.7 us: body(): jnp.einsum('zjk,ky->zjy', column_back, cas_y / total_y, precision=highest)]
    all_gather x2 -> x0, local copies, waits for them, and re-layouts: 44.2 us -> none  [body(): whole_plane = lax.all_gather(outlet, 'gy', axis=2, tiled=True)]
  transfers between devices with their start and end apart: 10 -> 10, of which waited for: 2 -> 3; matrix products, arithmetic and copies ran while one was open for 21% -> 24% of each run, Pallas kernels for 0% -> 0%
where the time goes in v1:
time: 1970 us; the launch traced here: 1960 us
  local copies, waits for them, and re-layouts  541 us (27%)
  other arithmetic  466 us (24%)
  waiting for transfers between devices  296 us (15%)
  blocking collectives  290 us (15%)
  Pallas kernels  252 us (13%)
  matrix products  80.5 us (4%)
  starting transfers between devices  20.2 us (1%)
    all_to_all x1, blocking collectives, solve_pressure(): return lax.all_to_all(back, 'gz', split_axis=0, concat_axis=0, tiled=True)  278 us
    all_to_all x1, waiting for transfers between devices, solve_pressure(): lax.all_to_all(spectral, 'gz', split_axis=0, concat_axis=0, tiled=True)  271 us
    pallas_call x1, Pallas kernels, solve_pressure(): pl.pallas_call(functools.partial(forward_kernel, block), grid=(per // blo...  132 us
    pallas_call x1, Pallas kernels, solve_pressure(): pl.pallas_call(functools.partial(backward_kernel, block), grid=(per // bl...  120 us
    add x1, other arithmetic, tendency(): return velocity + time_step * (eddy_visc * laplace - advect)  98.7 us
    unnamed x73, local copies, waits for them, and re-layouts  90.1 us
    mul x2, other arithmetic, tendency(): grad_y = 0.5 * (up_y - dn_y)  64 us
    slice x2, local copies, waits for them, and re-layouts, predict(): velocity[:, :, 1:]  49.2 us
  transfers between devices with their start and end apart: 10, of which 3 were waited for; matrix products, arithmetic and copies ran while one was open for 24% of the time, Pallas kernels for 0%

profile of v1, /device:TPU:0, one launch (start us, length us, event | category | flops | bytes accessed | tf_op | source)
XLA Modules:
  0.0 1960.2 jit_solution(11041658639201524004)
XLA Ops:
  7.2 27.7 %copy.264 = f32[3,48,128,384]{2,3,1,0:T(8,128)} copy(f32[3,48,128,384]{3,2,1,0:T(8,128)} %param.12) | data formatting | bytes 56623104 | tf_op args[1]
  36.2 9.6 copy.272
  50.0 6.4 collective-permute-start.3
  63.4 38.0 %fusion.175 = (f32[3,47,128,384]{2,3,1,0:T(8,128)}, f32[3,47,128,384]{2,3,1,0:T(8,128)}) fusion(f32[3,48,128,384]{2,3,1,0:T(8,128)} %copy.264), kind=kLoop, calls=%fused_computation.299 | loop fusion | bytes 110886912 | tf_op jit(solution)/shard_map/slice | solution.py:206
  101.5 38.0 %fusion.173 = (f32[3,48,128,383]{2,3,1,0:T(8,128)}, f32[3,48,128,383]{2,3,1,0:T(8,128)}) fusion(f32[3,48,128,384]{2,3,1,0:T(8,128)} %copy.264), kind=kLoop, calls=%fused_computation.297 | loop fusion | bytes 112951296 | tf_op jit(solution)/shard_map/jit(_roll_static)/slice | solution.py:209
  140.9 40.7 %fusion.172 = (f32[3,48,127,384]{2,3,1,0:T(8,128)}, f32[3,48,127,384]{2,3,1,0:T(8,128)}) fusion(f32[3,48,128,384]{2,3,1,0:T(8,128)} %copy.264), kind=kLoop, calls=%fused_computation.296 | loop fusion | bytes 112361472 | tf_op jit(solution)/shard_map/slice | solution.py:204
  181.6 23.5 %fusion.171 = (f32[1,48,128,384]{3,2,1,0:T(8,128)}, f32[48,128,384]{2,1,0:T(8,128)}, f32[48,128,384]{2,1,0:T(8,128)}, f32[48,128,384]{2,1,0:T(8,128)}) fusion(f32[3,48,128,384]{3,2,1,0:T(8,128)} %param.12), kind=kLoop, calls=%fused_computation.295 | loop fusion | flops 7077888 | bytes 66060288 | tf_op jit(solution)/shard_map/slice | solution.py:36
  205.8 8.1 fusion.182
  213.9 7.6 fusion.180
  221.6 8.5 fusion.178
  230.0 8.0 multiply_bitcast_fusion.5
  238.7 10.8 reshape_squeeze.7
  249.7 11.7 all_gather.9
  261.4 21.0 %gather_fusion = f32[512]{0:T(512)S(1)} fusion(f32[2359296]{0:T(1024)} %reshape_squeeze.7, s32[1024]{0:T(1024)S(1)} %pad_clamp_fusion), kind=kCustom, calls=%fused_computation | custom fusion | bytes 6144 | tf_op jit(solution)/shard_map/gather | solution.py:219
  283.0 11.4 fusion.39
  294.5 28.4 %fusion.3 = f32[3,48,128,384]{2,3,1,0:T(8,128)} fusion(f32[3,48,128,383]{2,3,1,0:T(8,128)} %get-tuple-element.63, f32[3,48,128,1]{2,3,1,0:T(1,128)S(1)} %get-tuple-element.65, f32[3,48,128,1]{2,3,1,0:T(1,128)S(1)} %get-tuple-element.64, f32[3,48,128,383]{2,3,1,0:T(8,128)} %get-tuple-element.62), kind=kLoop, calls=%fused_computation.15 | loop fusion | flops 28311552 | bytes 84934656 | tf_op jit(solution)/shard_map/mul | solution.py:32
  323.4 9.6 copy.284
  333.0 9.6 copy.285
  342.6 9.5 copy.286
  364.7 15.8 copy.278
  381.5 15.7 copy.280
  397.2 46.4 %broadcast_multiply_fusion = f32[3,48,128,384]{2,3,1,0:T(8,128)} fusion(f32[3,48,127,384]{2,3,1,0:T(8,128)} %get-tuple-element.61, f32[3,48,1,384]{2,3,1,0:T(8,128)} %copy.280, f32[3,48,1,384]{2,3,1,0:T(8,128)} %copy.278, f32[3,48,127,384]{2,3,1,0:T(8,128)} %get-tuple-element.60), kind=kLoop, calls=%fused_computation.16 | loop fusion | flops 28311552 | bytes 84934656 | tf_op jit(solution)/shard_map/mul | solution.py:33
  444.4 5.6 copy.257
  456.5 17.6 broadcast_multiply_fusion.1
  476.3 27.7 %fusion.1 = f32[3,48,128,384]{2,3,1,0:T(8,128)} fusion(f32[3,47,128,384]{2,3,1,0:T(8,128)} %get-tuple-element.67, f32[3,1,128,384]{2,3,1,0:T(8,128)S(1)} %slice.565, f32[3,1,128,384]{2,3,1,0:T(8,128)S(1)} %slice.564, f32[3,47,128,384]{2,3,1,0:T(8,128)} %get-tuple-element.66), kind=kLoop, calls=%fused_computation.13 | loop fusion | flops 28311552 | bytes 84934656 | tf_op jit(solution)/shard_map/mul | solution.py:34
  504.1 33.0 %fusion.13 = f32[48,128,384]{1,2,0:T(8,128)} fusion(f32[3,48,128,384]{2,3,1,0:T(8,128)} %broadcast_multiply_fusion, f32[3,48,128,384]{2,3,1,0:T(8,128)} %fusion.1, f32[3,48,128,384]{2,3,1,0:T(8,128)} %fusion.3), kind=kLoop, calls=%fused_computation.32 | loop fusion | flops 40108032 | bytes 94371840 | tf_op jit(solution)/shard_map/mul | solution.py:42
  537.1 98.7 %multiply_add_fusion = f32[3,48,128,384]{2,3,1,0:T(8,128)} fusion(f32[3,48,128,384]{2,3,1,0:T(8,128)} %copy.264, f32[3,47,128,384]{2,3,1,0:T(8,128)} %get-tuple-element.67, f32[3,1,128,384]{2,3,1,0:T(8,128)S(1)} %slice.565, f32[3,1,128,384]{2,3,1,0:T(8,128)S(1)} %slice.564, f32[3,47,128,384]{2,3,1,0:T(8,128)} %get-tuple-element.66, ...), kind=kLoop, calls=%fused_computation.11 | loop fusion | flops 176947200 | bytes 264241152 | tf_op jit(solution)/shard_map/add | solution.py:42
  635.8 8.4 slice.574
  644.2 12.7 slice.575
  656.9 9.6 copy.288
  666.5 10.7 reshape_squeeze.6
  677.2 11.4 scatter_fusion
  688.6 11.6 broadcast_in_dim_reshape.4
  700.2 9.6 copy.289
  709.8 13.8 add_multiply_fusion
  723.6 9.9 copy-done.2
  734.3 9.3 slice_reduce_fusion
  745.6 7.9 fusion.37
  754.3 7.1 fusion.49
  761.4 35.1 %add_multiply_fusion.1 = f32[3,48,128,128]{2,3,1,0:T(8,128)} fusion(f32[3,48,128,128]{2,3,1,0:T(8,128)} %copy.272, f32[3,47,128,128]{2,3,1,0:T(8,128)} %get-tuple-element.89, f32[3,1,128,128]{2,3,1,0:T(8,128)S(1)} %slice.539, f32[3,1,128,128]{2,3,1,0:T(8,128)S(1)} %slice.536, f32[3,47,128,128]{2,3,1,0:T(8,128)} %get-tuple-element.88, ...), kind=kLoop, calls=%fused_computation.74 | loop fusion | flops 61341696 | bytes 88080960 | tf_op jit(solution)/shard_map/mul | solution.py:247
  806.2 11.2 slice_bitcast_fusion.1
  817.4 11.7 slice_bitcast_fusion.3
  841.2 5.6 copy.292
  847.5 12.2 fusion.42
  860.6 35.0 %fusion.6 = f32[384,48,128]{2,0,1:T(8,128)} fusion(f32[3,48,128,384]{2,3,1,0:T(8,128)} %copy-done.2, f32[48,128,383]{1,2,0:T(8,128)} %bitcast.123, f32[48,128,1]{1,2,0:T(1,128)S(1)} %slice.585, f32[48,127,384]{1,2,0:T(8,128)} %bitcast.126, f32[48,1,384]{1,2,0:T(8,128)} %copy.292, f32[47,128,384]{1,2,0:T(8,128)} %slice_bitcast_fusion.3, ...), kind=kOutput, calls=%fused_computation.22 | convolution fusion | flops 10891984896 | bytes 66060288 | tf_op jit(solution)/shard_map/mx,zyx->mzy/dot_general | solution.py:263
  895.5 9.7 pad_maximum_fusion.7
  905.3 16.4 copy.294
  921.7 6.3 all-to-all-start
  930.2 270.8 %all-to-all-done = f32[512,48,128]{2,1,0:T(8,128)} async-done(((f32[512,48,128]{2,1,0:T(8,128)}), f32[512,48,128]{2,1,0:T(8,128)}, u32[]{:S(2)}, u32[]{:S(2)}) %all-to-all-start) | async-done | bytes 12582944 | tf_op jit(solution)/shard_map/all_to_all | solution.py:121
  1201.0 131.9 %solve_forward.1 = (f32[128,192,128]{2,1,0:T(8,128)}, f32[128,8,192]{2,1,0:T(8,128)S(1)}) custom-call(f32[128]{0:T(128)S(1)} %compare_select_fusion.5.rate_ref, f32[4,128,48,128]{3,2,1,0:T(8,128)} %bitcast.25.r_ref, f32[192,192]{1,0:T(8,128)S(1)} %get-tuple-element.103.dct_ref, f32[128,128]{1,0:T(8,128)S(1)} %scatter.10.dst_ref, ...), custom_call_target="tpu_custom_call" | custom-call | tf_op jit(solution)/shard_map/solve_forward/pallas_call | solution.py:138
  1334.7 24.3 %all-gather.3.cloned.1.call-done = f32[2048,192]{0,1:T(8,128)} async-done(((f32[256,192]{0,1:T(8,128)}), f32[2048,192]{0,1:T(8,128)}) %all-gather.3.cloned.1.call-update) | async-done | bytes 1572880 | tf_op jit(solution)/shard_map/all_gather | solution.py:151
  1363.4 120.4 %solve_backward.1 = f32[4,128,48,128]{3,2,1,0:T(8,128)} custom-call(f32[128]{0:T(128)S(1)} %compare_select_fusion.5.rate_ref, f32[128,192,128]{2,1,0:T(8,128)} %get-tuple-element.40.g_ref, f32[128,8,192]{2,1,0:T(8,128)S(1)} %concatenate.151.p_ref, f32[192,192]{1,0:T(8,128)S(1)} %get-tuple-element.102.dct_ref, f32[128,128]{1,0:T(8,128)S(1)} %scatter.10.dst_ref, ...), custom_call_target="tpu_custom_call" | custom-call | tf_op jit(solution)/shard_map/solve_backward/pallas_call | solution.py:173
  1483.8 278.0 %all_to_all.10 = f32[512,48,128]{2,1,0:T(8,128)S(1)} all-to-all(f32[512,48,128]{2,1,0:T(8,128)} %bitcast.122), channel_id=1, replica_groups=mesh['gz'=4,'gy'=8] {'gz'}, dimensions={0} | all-to-all | bytes 25165824 | tf_op jit(solution)/shard_map/all_to_all | solution.py:183
  1766.1 25.0 %fusion.34 = f32[48,128,384]{1,2,0:T(8,128)S(1)} fusion(f32[384,48,128]{2,1,0:T(8,128)} %slice.602), kind=kOutput, calls=%fused_computation.69 | convolution fusion | flops 10873257984 | bytes 18874368 | tf_op jit(solution)/shard_map/mzy,mx->zyx/dot_general | solution.py:275
  1802.0 7.6 copy.302
  1810.5 8.7 slice.608
  1819.2 6.1 slice.610
  1834.7 5.9 copy.308
  1843.7 27.4 %fusion.30 = (f32[1,48,128,384]{2,3,1,0:T(8,128)}, f32[1,48,128,384]{2,3,1,0:T(8,128)}, f32[1,48,128,384]{2,3,1,0:T(8,128)}) fusion(f32[48,128,384]{1,2,0:T(8,128)} %copy-done, f32[48,128,1]{1,2,0:T(1,128)S(1)} %slice.609, f32[48,128,383]{1,2,0:T(8,128)} %slice.608, f32[48,1,384]{1,2,0:T(8,128)} %copy.308, f32[48,127,384]{1,2,0:T(8,128)} %slice.610, ...), kind=kLoop, calls=%fused_computation.63 | loop fusion | flops 16515072 | bytes 66060480 | tf_op jit(solution)/shard_map/stack | solution.py:292
  1871.1 28.8 %maximum_subtract_fusion = f32[3,48,128,384]{2,3,1,0:T(8,128)} fusion(f32[1,48,128,384]{2,3,1,0:T(8,128)} %get-tuple-element.74, f32[1,48,128,384]{2,3,1,0:T(8,128)} %get-tuple-element.73, f32[1,48,128,384]{2,3,1,0:T(8,128)} %get-tuple-element.72, f32[3,48]{1,0:T(4,128)S(1)} %copy-done.17, f32[3,48,128]{2,1,0:T(8,128)S(1)} %bitcast.136, ...), kind=kLoop, calls=%fused_computation.9 | loop fusion | flops 56623104 | bytes 85010496 | tf_op jit(solution)/shard_map/sub | solution.py:292
  1900.0 27.9 %copy.313 = f32[3,48,128,384]{3,2,1,0:T(8,128)} copy(f32[3,48,128,384]{2,3,1,0:T(8,128)} %maximum_subtract_fusion) | data formatting | bytes 56623104
  1928.7 5.6 fusion.66
  1934.3 9.1 maximum_subtract_fusion.4
  1943.3 9.6 copy.312
  (185 shorter events, 104.3 us)
Async XLA Ops:
  47.8 426.4 %collective-permute-start.2 = (f32[3,1,128,512]{2,3,1,0:T(8,128)}, f32[3,1,128,512]{2,3,1,0:T(8,128)}, u32[]{:S(2)}, u32[]{:S(2)}) collective-permute-start(f32[3,1,128,512]{2,3,1,0:T(8,128)} %pad_maximum_fusion.14), channel_id=1, source_target_pairs={{8,0},{16,8},{24,16},{9,1},{17,9},{25,17},{10,2},{18,10},{26,18},{... | collective-permute-start | bytes 2359304 | tf_op jit(solution)/shard_map/ppermute | solution.py:28
  50.0 425.2 %collective-permute-start.3 = (f32[3,1,128,512]{2,3,1,0:T(8,128)}, f32[3,1,128,512]{2,3,1,0:T(8,128)}, u32[]{:S(2)}, u32[]{:S(2)}) collective-permute-start(f32[3,1,128,512]{2,3,1,0:T(8,128)} %pad_maximum_fusion.15), channel_id=1, source_target_pairs={{0,8},{8,16},{16,24},{1,9},{9,17},{17,25},{2,10},{10,18},{18,26},{... | collective-permute-start | bytes 2359304 | tf_op jit(solution)/shard_map/ppermute | solution.py:28
  60.9 302.8 %collective-permute-start = (f32[3,48,1,512]{3,1,2,0:T(8,128)}, f32[3,48,1,512]{3,1,2,0:T(8,128)}, u32[]{:S(2)}, u32[]{:S(2)}) collective-permute-start(f32[3,48,1,512]{3,1,2,0:T(8,128)} %pad_maximum_fusion.16), channel_id=1, source_target_pairs={{1,0},{2,1},{3,2},{4,3},{5,4},{6,5},{7,6},{0,7},{9,8},{10,9},{11,1... | collective-permute-start | bytes 884744 | tf_op jit(solution)/shard_map/ppermute | solution.py:22
  63.4 317.1 %collective-permute-start.1 = (f32[3,48,1,512]{3,1,2,0:T(8,128)}, f32[3,48,1,512]{3,1,2,0:T(8,128)}, u32[]{:S(2)}, u32[]{:S(2)}) collective-permute-start(f32[3,48,1,512]{3,1,2,0:T(8,128)} %pad_maximum_fusion.17), channel_id=1, source_target_pairs={{7,0},{0,1},{1,2},{2,3},{3,4},{4,5},{5,6},{6,7},{15,8},{8,9},{9,10... | collective-permute-start | bytes 884744 | tf_op jit(solution)/shard_map/ppermute | solution.py:22
  140.8 64.3 %slice-start = ((s8[9437184]{0:T(1024)(128)(4,1)}), s8[4194304]{0:T(1024)(128)(4,1)S(1)}, s32[]{:S(2)}) async-start(s8[9437184]{0:T(1024)(128)(4,1)} %bitcast.120), calls=%async_computation.3 | async-start | bytes 8388608
  140.8 64.2 %slice-start.1 = ((s8[9437184]{0:T(1024)(128)(4,1)}), s8[4194304]{0:T(1024)(128)(4,1)S(1)}, s32[]{:S(2)}) async-start(s8[9437184]{0:T(1024)(128)(4,1)} %bitcast.120), calls=%async_computation.4 | async-start | bytes 8388608
  181.6 23.5 %slice-start.2 = ((s8[9437184]{0:T(1024)(128)(4,1)}), s8[1048576]{0:T(1024)(128)(4,1)S(1)}, s32[]{:S(2)}) async-start(s8[9437184]{0:T(1024)(128)(4,1)} %bitcast.120), calls=%async_computation.5 | async-start | bytes 2097152
  205.2 77.8 %copy-start.7 = (f32[3,48,128,1]{2,3,1,0:T(1,128)}, f32[3,48,128,1]{2,3,1,0:T(1,128)S(1)}, u32[]{:S(2)}) copy-start(f32[3,48,128,1]{2,3,1,0:T(1,128)S(1)} %get-tuple-element.87) | copy-start | bytes 221188
  205.2 77.8 %copy-start.11 = (f32[3,48,128,1]{2,3,1,0:T(1,128)}, f32[3,48,128,1]{2,3,1,0:T(1,128)S(1)}, u32[]{:S(2)}) copy-start(f32[3,48,128,1]{2,3,1,0:T(1,128)S(1)} %get-tuple-element.86) | copy-start | bytes 221188
  230.0 8.0 copy-start.22
  238.1 0.6 copy-start.20
  238.7 10.9 copy-start.26
  352.1 9.4 copy-start.25
  666.5 10.7 copy-start.21
  666.5 10.7 copy-start.23
  700.2 9.6 copy-start.9
  700.2 9.6 copy-start.16
  700.2 9.6 copy-start.18
  723.6 10.0 copy-start.2
  734.3 19.2 slice-start.4
  745.5 8.0 slice-start.5
  745.5 8.8 slice-start.6
  754.3 7.1 copy-start.5
  817.4 19.1 copy-start.4
  817.4 11.7 copy-start.8
  817.4 15.0 copy-start.12
  829.8 17.0 collective-permute-start.5
  832.4 5.0 collective-permute-start.4
  837.4 0.6 copy-start.15
  846.8 0.7 copy-start.13
  860.6 35.0 %copy-start.6 = (f32[128,48,128]{2,0,1:T(8,128)S(1)}, f32[128,48,128]{2,0,1:T(8,128)}, u32[]{:S(2)}) copy-start(f32[128,48,128]{2,0,1:T(8,128)} %fusion.42) | copy-start | bytes 9437188
  921.7 279.3 %all-to-all-start = ((f32[512,48,128]{2,1,0:T(8,128)}), f32[512,48,128]{2,1,0:T(8,128)}, u32[]{:S(2)}, u32[]{:S(2)}) async-start(f32[512,48,128]{2,1,0:T(8,128)} %copy.294), calls=%async_computation | async-start | bytes 25165824 | tf_op jit(solution)/shard_map/all_to_all | solution.py:121
  928.0 431.0 %all-gather.3.cloned.1.call-start = ((), (), s32[]{:S(2)}) async-start(), calls=%async_computation.2 | async-start | bytes 1769472 | tf_op jit(solution)/shard_map/all_gather | solution.py:151
  1791.1 5.9 copy-start
  1795.6 38.4 %copy-start.3 = (f32[48,128,128]{1,2,0:T(8,128)}, f32[48,128,128]{1,2,0:T(8,128)S(1)}, u32[]{:S(2)}) copy-start(f32[48,128,128]{1,2,0:T(8,128)S(1)} %fusion.70) | copy-start | bytes 9437188
  1795.7 47.0 %collective-permute-start.7 = (f32[1,128,512]{1,2,0:T(8,128)S(1)}, f32[1,128,512]{1,2,0:T(8,128)}, u32[]{:S(2)}, u32[]{:S(2)}) collective-permute-start(f32[1,128,512]{1,2,0:T(8,128)S(1)} %pad_maximum_fusion.18), channel_id=1, source_target_pairs={{8,0},{16,8},{24,16},{9,1},{17,9},{25,17},{10,2},{18,10},{26,18},{... | collective-permute-start | bytes 786440 | tf_op jit(solution)/shard_map/ppermute | solution.py:28
  1809.5 24.5 %collective-permute-start.6 = (f32[48,1,512]{2,0,1:T(8,128)S(1)}, f32[48,1,512]{2,0,1:T(8,128)S(1)}, u32[]{:S(2)}, u32[]{:S(2)}) collective-permute-start(f32[48,1,512]{2,0,1:T(8,128)S(1)} %copy.302), channel_id=1, source_target_pairs={{1,0},{2,1},{3,2},{4,3},{5,4},{6,5},{7,6},{0,7},{9,8},{10,9},{11,1... | collective-permute-start | bytes 294920 | tf_op jit(solution)/shard_map/ppermute | solution.py:22
  1810.5 8.7 copy-start.1
  1834.0 0.6 copy-start.14
  1834.7 5.9 slice-start.7
  1843.7 27.4 %copy-start.10 = (f32[128,144,1]{0,1,2:T(8,128)S(1)}, f32[128,144,1]{0,1,2:T(8,128)}, u32[]{:S(2)}) copy-start(f32[128,144,1]{0,1,2:T(8,128)} %fusion.85) | copy-start | bytes 221188
  1843.7 27.4 %copy-start.17 = (f32[3,48]{1,0:T(4,128)S(1)}, f32[3,48]{1,0:T(4,128)}, u32[]{:S(2)}) copy-start(f32[3,48]{1,0:T(4,128)} %pad_convert_fusion) | copy-start | bytes 1732
  1843.7 27.4 %copy-start.19 = (f32[384]{0:T(512)S(1)}, f32[384]{0:T(512)}, u32[]{:S(2)}) copy-start(f32[384]{0:T(512)} %convert_multiply_fusion) | copy-start | bytes 4612
  1899.9 28.7 %slice-start.3 = ((f32[48,128,128]{1,2,0:T(8,128)}), f32[47,128,128]{1,2,0:T(8,128)S(1)}, s32[]{:S(2)}) async-start(f32[48,128,128]{1,2,0:T(8,128)} %copy-done.3), calls=%async_computation.6 | async-start | bytes 6160384 | tf_op jit(solution)/shard_map/slice | solution.py:290
  1899.9 28.7 %copy-start.24 = (f32[48]{0:T(128)S(1)}, f32[48]{0:T(128)}, u32[]{:S(2)}) copy-start(f32[48]{0:T(128)} %compare_convert_fusion) | copy-start | bytes 580
Sparse Core Ops, SparseCore 0:
  1334.1 24.8 all-gather.2
